TPU v7x, 32 devices: a whole 2x2x4 slice. The times are simulated.
32 devices in a mesh: group: 2 (over y), seq: 4 (over z), req: 2 (over x), sub: 2 (over core).
Axes of the slice: x: 2, y: 2, z: 4, core: 2. Of those that a mesh axis runs over, the one named last changes fastest.
Arguments:
- latent_codes: bfloat16 [2, 16, 2048, 512], P(None, ('group', 'req', 'sub'), 'seq'), parts along dimension 1, may hold values from -6 to 6
- latent_scales: bfloat16 [2, 16, 2048, 4], P(None, ('group', 'req', 'sub'), 'seq'), parts along dimension 1, may hold values from 0.34 to 3.5
- rope_keys: bfloat16 [2, 16, 2048, 64], P(None, ('group', 'req', 'sub'), 'seq'), parts along dimension 1, may hold values from -6 to 6
- lengths: int32 [16], P(('group', 'req', 'sub')), parts along dimension 0, may hold values from 256 to 2048, as said below
- query_latent: bfloat16 [2, 16, 4, 128, 512], P(None, ('group', 'req', 'sub'), None, 'seq'), parts along dimension 1, may hold values from -64 to 64
- query_rope: bfloat16 [2, 16, 4, 128, 64], P(None, ('group', 'req', 'sub'), None, 'seq'), parts along dimension 1, may hold values from -8 to 8
- new_latent: bfloat16 [2, 16, 4, 512], P(None, ('group', 'req', 'sub')), parts along dimension 1, may hold values from -9 to 9
- new_rope: bfloat16 [2, 16, 4, 64], P(None, ('group', 'req', 'sub')), parts along dimension 1, may hold values from -6 to 6
Outputs:
- attended: bfloat16 [2, 16, 4, 128, 512], P(None, ('group', 'req', 'sub'), None, 'seq'), parts along dimension 1
- cache_codes: bfloat16 [2, 16, 512, 4, 512], P(None, ('group', 'req', 'sub'), None, 'seq'), parts along dimension 1
- cache_scales: bfloat16 [2, 16, 512, 4, 4], P(None, ('group', 'req', 'sub'), None, 'seq'), parts along dimension 1
- cache_rope: bfloat16 [2, 16, 512, 4, 64], P(None, ('group', 'req', 'sub'), None, 'seq'), parts along dimension 1
There are 2 independent parts, one for each index of `group`. A program takes and returns all parts, laid end to end along the dimension named above; each array names one. Nothing has to cross between parts.
Inputs may be any that keep to these rules, and one draw needn't show every extreme that they name: `lengths`: one request is exactly 2048 long.
All inputs are finite; a program needn't handle non-finite values.
Results may differ from a plain program's by a relative error of at most 0.013.
Values may be sent and summed in bfloat16 or wider, within the bound.
A program may use at most 64 MiB of HBM per device.

v0:
```python
import jax
import jax.numpy as jnp
from jax import lax
from jax.sharding import PartitionSpec as P

softmax_gain = 192.0 ** (-0.5)
masked_score = -1e30


def dequantize(code_values, scale_values):
    blocks = scale_values.shape[-1]
    latent_width = code_values.shape[-1]
    shaped = code_values.astype(jnp.float32).reshape(
        code_values.shape[:-1] + (blocks, latent_width // blocks)
    )
    scaled = shaped * scale_values.astype(jnp.float32)[..., None]
    return scaled.reshape(code_values.shape).astype(jnp.bfloat16)


def shard_partial(
    lat_query, rope_query, key_rows, rope_rows, usable, new_keys, new_rope_rows, holds_new
):
    tokens_new, head_count, latent_width = lat_query.shape
    query_rows = lat_query.reshape(tokens_new * head_count, latent_width)
    query_pos = rope_query.reshape(tokens_new * head_count, rope_query.shape[-1])
    scores = jnp.dot(query_rows, key_rows.T, preferred_element_type=jnp.float32)
    scores = (
        scores + jnp.dot(query_pos, rope_rows.T, preferred_element_type=jnp.float32)
    ) * softmax_gain
    fresh_scores = jnp.dot(query_rows, new_keys.T, preferred_element_type=jnp.float32)
    fresh_scores = (
        fresh_scores + jnp.dot(query_pos, new_rope_rows.T, preferred_element_type=jnp.float32)
    ) * softmax_gain
    token_of_row = jnp.arange(tokens_new * head_count, dtype=jnp.int32) // head_count
    causal = (jnp.arange(tokens_new, dtype=jnp.int32)[None, :] <= token_of_row[:, None]) & holds_new
    scores = jnp.where(usable[None, :], scores, masked_score)
    fresh_scores = jnp.where(causal, fresh_scores, masked_score)
    group_peak = jnp.maximum(jnp.max(scores, 1), jnp.max(fresh_scores, 1)).astype(jnp.bfloat16)
    peak_float = group_peak.astype(jnp.float32)[:, None]
    weights = jnp.where(usable[None, :], jnp.exp(scores - peak_float), 0.0).astype(jnp.bfloat16)
    fresh_weights = jnp.where(causal, jnp.exp(fresh_scores - peak_float), 0.0).astype(jnp.bfloat16)
    group_total = jnp.sum(weights.astype(jnp.float32), 1) + jnp.sum(
        fresh_weights.astype(jnp.float32), 1
    )
    group_sum = jnp.dot(weights, key_rows, preferred_element_type=jnp.float32)
    group_sum = group_sum + jnp.dot(fresh_weights, new_keys, preferred_element_type=jnp.float32)
    return (
        group_sum.astype(jnp.bfloat16).reshape(tokens_new, head_count, latent_width),
        group_peak.reshape(tokens_new, head_count),
        group_total.astype(jnp.bfloat16).reshape(tokens_new, head_count),
    )


def merge_groups(pieces):
    group_sum, group_peak, group_total = pieces
    peak_float = group_peak.astype(jnp.float32)
    overall = jnp.max(peak_float, 0)
    factor = jnp.exp(peak_float - overall)
    numerator = jnp.sum(factor[..., None] * group_sum.astype(jnp.float32), 0)
    denominator = jnp.sum(factor * group_total.astype(jnp.float32), 0)
    return (numerator / denominator[..., None]).astype(jnp.bfloat16)


def per_device(
    latent_codes, latent_scales, rope_keys, lengths, query_latent, query_rope, new_latent, new_rope
):
    shard_count = lax.axis_size("seq")
    seq_index = lax.axis_index("seq")
    layer_count, request_count, span, latent_width = latent_codes.shape
    lat_query, rope_query = (
        lax.all_gather(query_latent, "seq", axis=3, tiled=True),
        lax.all_gather(query_rope, "seq", axis=3, tiled=True),
    )

    def regroup_rows(values):
        return values.reshape(
            values.shape[0], values.shape[1], span // shard_count, shard_count, values.shape[-1]
        )

    codes_moved, scales_moved, rope_moved = (
        lax.all_to_all(regroup_rows(latent_codes), "seq", split_axis=3, concat_axis=2, tiled=True),
        lax.all_to_all(regroup_rows(latent_scales), "seq", split_axis=3, concat_axis=2, tiled=True),
        lax.all_to_all(regroup_rows(rope_keys), "seq", split_axis=3, concat_axis=2, tiled=True),
    )
    offsets = jnp.arange(span, dtype=jnp.int32)
    key_rows = dequantize(latent_codes, latent_scales)
    positions = seq_index * span + offsets
    usable = positions[None, :] < lengths[:, None]
    holds_new = seq_index == 0
    per_request = jax.vmap(shard_partial, in_axes=(0, 0, 0, 0, 0, 0, 0, None))
    per_layer = jax.vmap(per_request, in_axes=(0, 0, 0, 0, None, 0, 0, None))
    group_sum, group_peak, group_total = per_layer(
        lat_query, rope_query, key_rows, rope_keys, usable, new_latent, new_rope, holds_new
    )
    attended = merge_groups(
        (
            lax.all_to_all(group_sum[None], "seq", split_axis=4, concat_axis=0, tiled=True),
            lax.all_to_all(group_peak[None], "seq", split_axis=4, concat_axis=0, tiled=True),
            lax.all_to_all(group_total[None], "seq", split_axis=4, concat_axis=0, tiled=True),
        )
    )
    return (attended, codes_moved, scales_moved, rope_moved)


def solution(mesh):
    placed = (
        P(None, ("group", "req", "sub"), "seq", None),
        P(None, ("group", "req", "sub"), "seq", None),
        P(None, ("group", "req", "sub"), "seq", None),
        P(("group", "req", "sub")),
        P(None, ("group", "req", "sub"), None, "seq", None),
        P(None, ("group", "req", "sub"), None, "seq", None),
        P(None, ("group", "req", "sub"), None, None),
        P(None, ("group", "req", "sub"), None, None),
    )
    return jax.shard_map(
        per_device,
        mesh=mesh,
        in_specs=placed,
        out_specs=(
            P(None, ("group", "req", "sub"), None, "seq", None),
            P(None, ("group", "req", "sub"), None, "seq", None),
            P(None, ("group", "req", "sub"), None, "seq", None),
            P(None, ("group", "req", "sub"), None, "seq", None),
        ),
        check_vma=False,
    )
```

profile of v0, /device:TPU:0, one launch (start us, length us, event | category | flops | bytes accessed | tf_op | source)
XLA Modules:
  0.0 215.6 jit_solution(11127280630018597931)
XLA Ops:
  7.9 1.8 reshape.126
  10.6 6.3 %all-to-all-start.4 = ((bf16[2,2,128,4,4]{2,4,1,0,3:T(4,128)(2,1)}), bf16[2,2,128,4,4]{2,4,1,0,3:T(4,128)(2,1)S(1)}, u32[]{:S(2)}, u32[]{:S(2)}) async-start(bf16[2,2,128,4,4]{2,4,1,0,3:T(4,128)(2,1)} %copy.66), calls=%async_computation.4 | async-start | bytes 32768 | tf_op jit(solution)/shard_map/all_to_all | solution.py:82
  19.2 3.4 %all-to-all-done.4 = bf16[2,2,128,4,4]{2,4,1,0,3:T(4,128)(2,1)S(1)} async-done(((bf16[2,2,128,4,4]{2,4,1,0,3:T(4,128)(2,1)}), bf16[2,2,128,4,4]{2,4,1,0,3:T(4,128)(2,1)S(1)}, u32[]{:S(2)}, u32[]{:S(2)}) %all-to-all-start.4) | async-done | bytes 16416 | tf_op jit(solution)/shard_map/all_to_all | solution.py:82
  22.5 3.4 %all-to-all-start.5 = ((bf16[2,2,128,4,64]{2,4,1,0,3:T(8,128)(2,1)}), bf16[2,2,128,4,64]{2,4,1,0,3:T(8,128)(2,1)S(1)}, u32[]{:S(2)}, u32[]{:S(2)}) async-start(bf16[2,2,128,4,64]{2,4,1,0,3:T(8,128)(2,1)} %copy.69), calls=%async_computation.5 | async-start | bytes 524288 | tf_op jit(solution)/shard_map/all_to_all | solution.py:83
  26.9 3.9 %mul.38 = f32[2,2,512,4,128]{4,3,2,1,0:T(4,128)} broadcast(f32[2,2,512,4]{3,2,1,0:T(8,128)S(1)} %copy.57), dimensions={0,1,2,3} | broadcast | bytes 4227072 | tf_op jit(solution)/shard_map/mul | solution.py:16
  30.8 5.6 %mul.39 = f32[2,2,512,512]{3,2,1,0:T(8,128)} reshape(f32[2,2,512,4,128]{4,3,2,1,0:T(4,128)} %mul.38) | data formatting | bytes 8388608 | tf_op jit(solution)/shard_map/mul | solution.py:16
  36.4 2.2 %copy.63 = bf16[2,2,512,512]{3,1,2,0:T(2,128)(2,1)S(1)} copy(bf16[2,2,512,512]{3,2,1,0:T(8,128)(2,1)S(1)} %copy-done.2) | data formatting | bytes 4194304 | tf_op args[0]
  38.6 2.0 copy.64
  40.6 1.7 all-to-all-done.5
  42.3 4.5 %all-to-all-start.3 = ((bf16[2,2,128,4,512]{4,2,1,0,3:T(8,128)(2,1)}), bf16[2,2,128,4,512]{4,2,1,0,3:T(8,128)(2,1)}, u32[]{:S(2)}, u32[]{:S(2)}) async-start(bf16[2,2,128,4,512]{4,2,1,0,3:T(8,128)(2,1)} %copy.64), calls=%async_computation.3 | async-start | bytes 4194304 | tf_op jit(solution)/shard_map/all_to_all | solution.py:81
  46.8 71.2 %all_gather.7 = bf16[2,2,4,128,64]{4,3,2,1,0:T(8,128)(2,1)S(1)} all-gather(bf16[2,2,4,32,64]{4,3,2,1,0:T(8,128)(2,1)S(1)} %copy-done.4), channel_id=1, replica_groups=mesh['group'=2,'seq'=4,'req'=2,'sub'=2] {'seq'}, dimensions={3}, use_global_device_ids=true | all-gather | bytes 327680 | tf_op jit(solution)/shard_map/all_gather | solution.py:72
  118.3 2.8 %fusion.16 = f32[2,2,512,512]{2,3,1,0:T(8,128)} fusion(bf16[2,2,512,64]{3,2,1,0:T(8,128)(2,1)S(1)} %bitcast.77, bf16[2,2,512,64]{2,3,1,0:T(8,128)(2,1)S(1)} %copy-done.3), kind=kOutput, calls=%fused_computation.39 | convolution fusion | flops 134217728 | bytes 4718592 | tf_op jit(solution)/shard_map/vmap(vmap())/dot_general | solution.py:28
  121.1 2.3 %fusion.15 = (bf16[2,2,512]{2,1,0:T(2,128)(2,1)S(1)}, f32[2,2,512,4]{2,3,1,0:T(4,128)S(1)}) fusion(f32[2,2,512,4]{2,3,1,0:T(4,128)S(1)} %fusion.17, bf16[2,2,512,512]{3,2,1,0:T(8,128)(2,1)} %bitcast.74, bf16[2,2,4,512]{3,2,1,0:T(4,128)(2,1)S(1)} %copy-done, pred[512,4]{0,1:T(4,128)(4,1)S(1)} %fusion.8), kind=kOutput, calls=%fused_computation.38 | convolution fusion | flops 8419328 | bytes 2185216 | tf_op jit(solution)/shard_map/vmap(vmap())/dot_general | solution.py:30
  123.4 5.6 %fusion.14 = (bf16[2,2,512]{2,1,0:T(2,128)(2,1)S(1)}, f32[2,2,512,512]{2,3,1,0:T(8,128)S(1)}) fusion(f32[2,2,512,512]{2,3,1,0:T(8,128)} %fusion.16, bf16[2,2,512,512]{3,2,1,0:T(8,128)(2,1)} %bitcast.75, f32[2,2,512,512]{3,2,1,0:T(8,128)} %mul.39, bf16[2,2,512,512]{3,2,1,0:T(8,128)(2,1)S(1)} %copy-done.2, pred[2,512]{1,0:T(4,128)(4,1)S(1)} %broadcast_compare_fusion), kind=kOutput, calls=%fused_computation.37 | convolution fusion | flops 1081079808 | bytes 16782336 | tf_op jit(solution)/shard_map/vmap(vmap())/dot_general | solution.py:26
  129.0 1.9 copy-done.1
  132.7 5.0 %all-to-all-start.2 = ((bf16[4,2,256]{2,1,0:T(2,128)(2,1)}), bf16[4,2,256]{2,1,0:T(2,128)(2,1)S(1)}, u32[]{:S(2)}, u32[]{:S(2)}) async-start(bf16[4,2,256]{2,1,0:T(2,128)(2,1)} %reshape.135), calls=%async_computation.2 | async-start | bytes 8192 | tf_op jit(solution)/shard_map/all_to_all | solution.py:99
  137.6 7.1 %fusion.5 = f32[2,2,512,512]{3,2,1,0:T(8,128)} fusion(f32[2,2,512,512]{2,3,1,0:T(8,128)} %copy-done.1, f32[2,2,512]{2,1,0:T(2,128)S(1)} %get-tuple-element.20, pred[2,512]{1,0:T(4,128)(4,1)S(1)} %broadcast_compare_fusion, f32[2,2,512,512]{3,2,1,0:T(8,128)} %mul.39, bf16[2,2,512,512]{3,2,1,0:T(8,128)(2,1)S(1)} %copy-done.2), kind=kOutput, calls=%fused_computation.13 | convolution fusion | flops 1080033280 | bytes 14689280 | tf_op jit(solution)/shard_map/vmap(vmap())/dot_general | solution.py:45
  145.7 5.1 %all-to-all-start = ((bf16[4,2,256]{2,1,0:T(2,128)(2,1)}), bf16[4,2,256]{2,1,0:T(2,128)(2,1)S(1)}, u32[]{:S(2)}, u32[]{:S(2)}) async-start(bf16[4,2,256]{2,1,0:T(2,128)(2,1)} %reshape.133), calls=%async_computation | async-start | bytes 8192 | tf_op jit(solution)/shard_map/all_to_all | solution.py:98
  150.8 3.0 %add_convert_fusion = bf16[2,2,512,512]{3,2,1,0:T(8,128)(2,1)S(1)} fusion(f32[2,2,512,512]{3,2,1,0:T(8,128)} %fusion.5, bf16[2,2,4,512]{3,2,1,0:T(4,128)(2,1)S(1)} %copy-done, f32[2,2,512,4]{2,3,1,0:T(4,128)S(1)} %get-tuple-element.27, f32[2,2,512]{2,1,0:T(2,128)S(1)} %get-tuple-element.20, pred[512,4]{0,1:T(4,128)(4,1)S(1)} %fusion.8), kind=kOutput, calls=%fused_computation.6 | convolution fusion | flops 10510336 | bytes 6350848 | tf_op jit(solution)/shard_map/vmap(vmap())/dot_general | solution.py:46
  153.8 3.0 %copy.61 = bf16[1,2,2,4,128,512]{5,3,2,1,0,4:T(4,128)(2,1)} copy(bf16[1,2,2,4,128,512]{5,4,3,2,1,0:T(8,128)(2,1)S(1)} %bitcast.72) | data formatting | bytes 4194304 | tf_op jit(solution)/shard_map/broadcast_in_dim;vmap(vmap())/reshape | solution.py:97
  156.8 5.1 %all-to-all-start.1 = ((bf16[1,2,2,4,128,512]{5,3,2,1,0,4:T(4,128)(2,1)}), bf16[1,2,2,4,128,512]{5,3,2,1,0,4:T(4,128)(2,1)S(1)}, u32[]{:S(2)}, u32[]{:S(2)}) async-start(bf16[1,2,2,4,128,512]{5,3,2,1,0,4:T(4,128)(2,1)} %copy.61), calls=%async_computation.1 | async-start | bytes 4194304 | tf_op jit(solution)/shard_map/all_to_all | solution.py:97
  163.2 3.1 %copy.65 = bf16[2,2,128,4,512]{4,2,3,1,0:T(8,128)(2,1)} copy(bf16[2,2,128,4,512]{4,2,1,0,3:T(8,128)(2,1)} %all-to-all-done.3) | data formatting | bytes 4194304 | tf_op jit(solution)/shard_map/all_to_all | solution.py:81
  167.4 38.4 %all-to-all-done.1 = bf16[1,2,2,4,128,512]{5,3,2,1,0,4:T(4,128)(2,1)S(1)} async-done(((bf16[1,2,2,4,128,512]{5,3,2,1,0,4:T(4,128)(2,1)}), bf16[1,2,2,4,128,512]{5,3,2,1,0,4:T(4,128)(2,1)S(1)}, u32[]{:S(2)}, u32[]{:S(2)}) %all-to-all-start.1) | async-done | bytes 2097184 | tf_op jit(solution)/shard_map/all_to_all | solution.py:97
  205.9 1.5 fusion
  (47 shorter events, 11.7 us)
Async XLA Ops:
  7.2 113.9 %copy-start = (bf16[2,2,4,512]{3,2,1,0:T(4,128)(2,1)S(1)}, bf16[2,2,4,512]{3,2,1,0:T(4,128)(2,1)}, u32[]{:S(2)}) copy-start(bf16[2,2,4,512]{3,2,1,0:T(4,128)(2,1)} %param.14) | copy-start | bytes 49156
  7.2 113.9 %all-gather.2.cloned.1.call-start = ((), (), s32[]{:S(2)}) async-start(), calls=%async_computation.6 | async-start | bytes 2621440 | tf_op jit(solution)/shard_map/all_gather | solution.py:71
  10.6 11.9 %all-to-all-start.4 = ((bf16[2,2,128,4,4]{2,4,1,0,3:T(4,128)(2,1)}), bf16[2,2,128,4,4]{2,4,1,0,3:T(4,128)(2,1)S(1)}, u32[]{:S(2)}, u32[]{:S(2)}) async-start(bf16[2,2,128,4,4]{2,4,1,0,3:T(4,128)(2,1)} %copy.66), calls=%async_computation.4 | async-start | bytes 32768 | tf_op jit(solution)/shard_map/all_to_all | solution.py:82
  22.5 19.8 %all-to-all-start.5 = ((bf16[2,2,128,4,64]{2,4,1,0,3:T(8,128)(2,1)}), bf16[2,2,128,4,64]{2,4,1,0,3:T(8,128)(2,1)S(1)}, u32[]{:S(2)}, u32[]{:S(2)}) async-start(bf16[2,2,128,4,64]{2,4,1,0,3:T(8,128)(2,1)} %copy.69), calls=%async_computation.5 | async-start | bytes 524288 | tf_op jit(solution)/shard_map/all_to_all | solution.py:83
  30.8 5.6 %copy-start.2 = (bf16[2,2,512,512]{3,2,1,0:T(8,128)(2,1)S(1)}, bf16[2,2,512,512]{3,2,1,0:T(8,128)(2,1)}, u32[]{:S(2)}) copy-start(bf16[2,2,512,512]{3,2,1,0:T(8,128)(2,1)} %param.8) | copy-start | bytes 6291460
  38.6 8.2 %copy-start.4 = (bf16[2,2,4,32,64]{4,3,2,1,0:T(8,128)(2,1)S(1)}, bf16[2,2,4,32,64]{4,3,2,1,0:T(8,128)(2,1)}, u32[]{:S(2)}) copy-start(bf16[2,2,4,32,64]{4,3,2,1,0:T(8,128)(2,1)} %param.13) | copy-start | bytes 196612
  38.6 79.4 %copy-start.6 = (s32[2]{0:T(128)S(1)}, s32[2]{0:T(128)}, u32[]{:S(2)}) copy-start(s32[2]{0:T(128)} %param.11) | copy-start | bytes 28
  38.6 79.5 %copy-start.5 = (bf16[2,2,4,64]{3,2,1,0:T(4,128)(2,1)S(1)}, bf16[2,2,4,64]{3,2,1,0:T(4,128)(2,1)}, u32[]{:S(2)}) copy-start(bf16[2,2,4,64]{3,2,1,0:T(4,128)(2,1)} %param.15) | copy-start | bytes 6148
  38.6 79.7 %copy-start.3 = (bf16[2,2,512,64]{2,3,1,0:T(8,128)(2,1)S(1)}, bf16[2,2,512,64]{2,3,1,0:T(8,128)(2,1)}, u32[]{:S(2)}) copy-start(bf16[2,2,512,64]{2,3,1,0:T(8,128)(2,1)} %param.10) | copy-start | bytes 786436
  42.3 90.3 %all-to-all-start.3 = ((bf16[2,2,128,4,512]{4,2,1,0,3:T(8,128)(2,1)}), bf16[2,2,128,4,512]{4,2,1,0,3:T(8,128)(2,1)}, u32[]{:S(2)}, u32[]{:S(2)}) async-start(bf16[2,2,128,4,512]{4,2,1,0,3:T(8,128)(2,1)} %copy.64), calls=%async_computation.3 | async-start | bytes 4194304 | tf_op jit(solution)/shard_map/all_to_all | solution.py:81
  128.9 2.0 copy-start.1
  132.7 13.1 %all-to-all-start.2 = ((bf16[4,2,256]{2,1,0:T(2,128)(2,1)}), bf16[4,2,256]{2,1,0:T(2,128)(2,1)S(1)}, u32[]{:S(2)}, u32[]{:S(2)}) async-start(bf16[4,2,256]{2,1,0:T(2,128)(2,1)} %reshape.135), calls=%async_computation.2 | async-start | bytes 8192 | tf_op jit(solution)/shard_map/all_to_all | solution.py:99
  145.7 11.0 %all-to-all-start = ((bf16[4,2,256]{2,1,0:T(2,128)(2,1)}), bf16[4,2,256]{2,1,0:T(2,128)(2,1)S(1)}, u32[]{:S(2)}, u32[]{:S(2)}) async-start(bf16[4,2,256]{2,1,0:T(2,128)(2,1)} %reshape.133), calls=%async_computation | async-start | bytes 8192 | tf_op jit(solution)/shard_map/all_to_all | solution.py:98
  156.8 49.1 %all-to-all-start.1 = ((bf16[1,2,2,4,128,512]{5,3,2,1,0,4:T(4,128)(2,1)}), bf16[1,2,2,4,128,512]{5,3,2,1,0,4:T(4,128)(2,1)S(1)}, u32[]{:S(2)}, u32[]{:S(2)}) async-start(bf16[1,2,2,4,128,512]{5,3,2,1,0,4:T(4,128)(2,1)} %copy.61), calls=%async_computation.1 | async-start | bytes 4194304 | tf_op jit(solution)/shard_map/all_to_all | solution.py:97
Sparse Core Ops, SparseCore 0:
  9.6 73.4 all-gather.1
where the time goes:
time: 216 us
  blocking collectives  71.2 us (33%)
  waiting for transfers between devices  44.2 us (20%)
  local copies, waits for them, and re-layouts  32.4 us (15%)
  starting transfers between devices  29.4 us (14%)
  matrix products  20.9 us (10%)
  between operations  14.3 us (7%)
  other arithmetic  3.24 us (2%)
    all_gather x1, blocking collectives, per_device(): lax.all_gather(query_rope, 'seq', axis=3, tiled=True)  71.2 us
    all_to_all x1, waiting for transfers between devices, per_device(): lax.all_to_all(group_sum[None], 'seq', split_axis=4, concat_axis=0, tiled...  38.4 us
    mul x2, local copies, waits for them, and re-layouts, dequantize(): scaled = shaped * scale_values.astype(jnp.float32)[..., None]  9.47 us
    unnamed x22, local copies, waits for them, and re-layouts  9.29 us
    dot_general x1, matrix products, shard_partial(): group_sum = jnp.dot(weights, key_rows, preferred_element_type=jnp.float32)  7.14 us
    all_to_all x1, starting transfers between devices, per_device(): lax.all_to_all(regroup_rows(latent_scales), 'seq', split_axis=3, concat_a...  6.32 us
    reshape x4, local copies, waits for them, and re-layouts, regroup_rows(): values.reshape(values.shape[0], values.shape[1], span // shard_count, sha...  5.68 us
    dot_general x1, matrix products, shard_partial(): scores = jnp.dot(query_rows, key_rows.T, preferred_element_type=jnp.float32)  5.57 us
  transfers between devices with their start and end apart: 7, of which 3 were waited for; matrix products, arithmetic and copies ran while one was open for 24% of the time, Pallas kernels for 0%

commit v1 on v0

--- a/solution.py
+++ b/solution.py
@@ -5,6 +5,27 @@
 
 softmax_gain = 192.0 ** (-0.5)
 masked_score = -1e30
+
+
+def collect(x, axis, dim):
+    peers, place, rows = (lax.axis_size(axis), lax.axis_index(axis), x.shape[dim])
+    right = [(i, (i + 1) % peers) for i in range(peers)]
+    left = [(i, (i - 1) % peers) for i in range(peers)]
+    whole = jnp.zeros((*x.shape[:dim], peers * rows, *x.shape[dim + 1 :]), x.dtype)
+    whole = lax.dynamic_update_slice_in_dim(whole, x, place * rows, axis=dim)
+    from_left = from_right = x
+    middle = peers // 2
+    for step in range(1, middle + 1):
+        from_left = lax.ppermute(from_left, axis, right)
+        whole = lax.dynamic_update_slice_in_dim(
+            whole, from_left, (place - step) % peers * rows, axis=dim
+        )
+        if step < peers - middle:
+            from_right = lax.ppermute(from_right, axis, left)
+            whole = lax.dynamic_update_slice_in_dim(
+                whole, from_right, (place + step) % peers * rows, axis=dim
+            )
+    return whole
 
 
 def dequantize(code_values, scale_values):
@@ -69,7 +90,7 @@
     layer_count, request_count, span, latent_width = latent_codes.shape
     lat_query, rope_query = (
         lax.all_gather(query_latent, "seq", axis=3, tiled=True),
-        lax.all_gather(query_rope, "seq", axis=3, tiled=True),
+        collect(query_rope, "seq", 3),
     )
 
     def regroup_rows(values):

time: 216 us -> 357 us (1.65)
  local copies, waits for them, and re-layouts: 32.4 us -> 169 us
  blocking collectives: 71.2 us -> 0 us
  waiting for transfers between devices: 44.2 us -> 106 us
  starting transfers between devices: 29.4 us -> 43.8 us
    dynamic_update_slice x0 -> x4, local copies, waits for them, and re-layouts: none -> 133 us  [the longest x2 84 us: collect(): lax.dynamic_update_slice_in_dim(whole, from_left, (place - step) % peers...]
    all_gather x1 -> x0, blocking collectives: 71.2 us -> none  [per_device(): lax.all_gather(query_rope, 'seq', axis=3, tiled=True)]
    ppermute x0 -> x3, waiting for transfers between devices: none -> 49.1 us  [the longest x2 49.1 us: collect(): from_left = lax.ppermute(from_left, axis, right)]
    ppermute x0 -> x3, starting transfers between devices: none -> 15.5 us  [the longest x2 13.6 us: collect(): from_left = lax.ppermute(from_left, axis, right)]
    all_to_all x1, waiting for transfers between devices: 1.7 us -> 12.2 us  [per_device(): lax.all_to_all(regroup_rows(rope_keys), 'seq', split_axis=3, concat_axis=...]
    unnamed x22 -> x35, local copies, waits for them, and re-layouts: 9.29 us -> 9.5 us
  transfers between devices with their start and end apart: 7 -> 10, of which waited for: 3 -> 4; matrix products, arithmetic and copies ran while one was open for 24% -> 53% of each run, Pallas kernels for 0% -> 0%
where the time goes in v1:
time: 357 us; the launch traced here: 356 us
  local copies, waits for them, and re-layouts  169 us (47%)
  waiting for transfers between devices  106 us (30%)
  starting transfers between devices  43.8 us (12%)
  matrix products  18 us (5%)
  between operations  14.5 us (4%)
  other arithmetic  4.41 us (1%)
    dynamic_update_slice x2, local copies, waits for them, and re-layouts, collect(): lax.dynamic_update_slice_in_dim(whole, from_left, (place - step) % peers...  84 us
    ppermute x2, waiting for transfers between devices, collect(): from_left = lax.ppermute(from_left, axis, right)  49.1 us
    dynamic_update_slice x1, local copies, waits for them, and re-layouts, collect(): lax.dynamic_update_slice_in_dim(whole, from_right, (place + step) % peers...  42 us
    all_to_all x1, waiting for transfers between devices, per_device(): lax.all_to_all(group_sum[None], 'seq', split_axis=4, concat_axis=0, tiled...  40.6 us
    ppermute x2, starting transfers between devices, collect(): from_left = lax.ppermute(from_left, axis, right)  13.6 us
    all_to_all x1, waiting for transfers between devices, per_device(): lax.all_to_all(regroup_rows(rope_keys), 'seq', split_axis=3, concat_axis=...  12.2 us
    unnamed x35, local copies, waits for them, and re-layouts  9.5 us
    mul x2, local copies, waits for them, and re-layouts, dequantize(): scaled = shaped * scale_values.astype(jnp.float32)[..., None]  9.33 us
  transfers between devices with their start and end apart: 10, of which 4 were waited for; matrix products, arithmetic and copies ran while one was open for 53% of the time, Pallas kernels for 0%

profile of v1, /device:TPU:0, one launch (start us, length us, event | category | flops | bytes accessed | tf_op | source)
XLA Modules:
  0.0 356.1 jit_solution(3393466715288613389)
XLA Ops:
  10.6 6.3 %all-to-all-start.4 = ((bf16[2,2,128,4,4]{2,4,1,0,3:T(4,128)(2,1)}), bf16[2,2,128,4,4]{2,4,1,0,3:T(4,128)(2,1)S(1)}, u32[]{:S(2)}, u32[]{:S(2)}) async-start(bf16[2,2,128,4,4]{2,4,1,0,3:T(4,128)(2,1)} %copy.84), calls=%async_computation.4 | async-start | bytes 32768 | tf_op jit(solution)/shard_map/all_to_all | solution.py:103
  19.2 3.4 all-to-all-done.4
  22.5 3.4 all-to-all-start.5
  26.0 2.2 copy.81
  30.1 12.2 %all-to-all-done.5 = bf16[2,2,128,4,64]{2,4,1,0,3:T(8,128)(2,1)S(1)} async-done(((bf16[2,2,128,4,64]{2,4,1,0,3:T(8,128)(2,1)}), bf16[2,2,128,4,64]{2,4,1,0,3:T(8,128)(2,1)S(1)}, u32[]{:S(2)}, u32[]{:S(2)}) %all-to-all-start.5) | async-done | bytes 262176 | tf_op jit(solution)/shard_map/all_to_all | solution.py:104
  42.3 4.5 %all-to-all-start.3 = ((bf16[2,2,128,4,512]{4,2,1,0,3:T(8,128)(2,1)}), bf16[2,2,128,4,512]{4,2,1,0,3:T(8,128)(2,1)}, u32[]{:S(2)}, u32[]{:S(2)}) async-start(bf16[2,2,128,4,512]{4,2,1,0,3:T(8,128)(2,1)} %copy.82), calls=%async_computation.3 | async-start | bytes 4194304 | tf_op jit(solution)/shard_map/all_to_all | solution.py:102
  51.4 49.1 %collective-permute-done = bf16[2,2,4,32,64]{4,3,2,1,0:T(8,128)(2,1)} collective-permute-done((bf16[2,2,4,32,64]{4,3,2,1,0:T(8,128)(2,1)S(1)}, bf16[2,2,4,32,64]{4,3,2,1,0:T(8,128)(2,1)}, u32[]{:S(2)}, u32[]{:S(2)}) %collective-permute-start) | collective-permute-done | bytes 65568 | tf_op jit(solution)/shard_map/ppermute | solution.py:19
  100.4 11.7 %collective-permute-start.2 = (bf16[2,2,4,32,64]{4,3,2,1,0:T(8,128)(2,1)}, bf16[2,2,4,32,64]{4,3,2,1,0:T(8,128)(2,1)}, u32[]{:S(2)}, u32[]{:S(2)}) collective-permute-start(bf16[2,2,4,32,64]{4,3,2,1,0:T(8,128)(2,1)} %collective-permute-done), channel_id=1, source_target_pairs={{0,4},{4,8},{8,12},{12,0},{1,5},{5,9},{9,13},{13,1},{2,6},{6,10},{... | collective-permute-start | bytes 196616 | tf_op jit(solution)/shard_map/ppermute | solution.py:19
  113.9 3.9 %mul.50 = f32[2,2,512,4,128]{4,3,2,1,0:T(4,128)} broadcast(f32[2,2,512,4]{3,2,1,0:T(8,128)S(1)} %copy.72), dimensions={0,1,2,3} | broadcast | bytes 4227072 | tf_op jit(solution)/shard_map/mul | solution.py:37
  117.8 5.5 %mul.51 = f32[2,2,512,512]{3,2,1,0:T(8,128)} reshape(f32[2,2,512,4,128]{4,3,2,1,0:T(4,128)} %mul.50) | data formatting | bytes 8388608 | tf_op jit(solution)/shard_map/mul | solution.py:37
  123.3 7.5 %dynamic_update_slice.12 = bf16[2,2,4,128,64]{3,2,4,1,0:T(4,128)(2,1)S(1)} dynamic-update-slice(bf16[2,2,4,128,64]{3,2,4,1,0:T(4,128)(2,1)S(1)} %broadcast_in_dim.45, bf16[2,2,4,32,64]{3,2,4,1,0:T(4,128)(2,1)S(1)} %copy.73, s32[]{:T(128)} %constant.52.clone.1, s32[]{:T(128)} %constant.52.clone.1, s32[]{:T(128)} %constant.52.clone.1, s32[]{:T(128)S(6)} %select_n.50, s32[]{:T(128)} %constant.52.clone.1) | dynamic-update-slice | bytes 131076 | tf_op jit(solution)/shard_map/dynamic_update_slice | solution.py:15
  131.9 42.0 %dynamic_update_slice.13 = bf16[2,2,4,128,64]{3,2,4,1,0:T(4,128)(2,1)S(1)} dynamic-update-slice(bf16[2,2,4,128,64]{3,2,4,1,0:T(4,128)(2,1)S(1)} %dynamic_update_slice.12, bf16[2,2,4,32,64]{3,2,4,1,0:T(4,128)(2,1)S(1)} %copy.74, s32[]{:T(128)} %constant.52.clone.1, s32[]{:T(128)} %constant.52.clone.1, s32[]{:T(128)} %constant.52.clone.1, s32[]{:T(128)S(6)} %select_n.52, s32[]{:T(128)} %constant.52.clone.1) | dynamic-update-slice | bytes 131076 | tf_op jit(solution)/shard_map/dynamic_update_slice | solution.py:20
  175.0 42.0 %dynamic_update_slice.14 = bf16[2,2,4,128,64]{3,2,4,1,0:T(4,128)(2,1)S(1)} dynamic-update-slice(bf16[2,2,4,128,64]{3,2,4,1,0:T(4,128)(2,1)S(1)} %dynamic_update_slice.13, bf16[2,2,4,32,64]{3,2,4,1,0:T(4,128)(2,1)S(1)} %copy.75, s32[]{:T(128)} %constant.52.clone.1, s32[]{:T(128)} %constant.52.clone.1, s32[]{:T(128)} %constant.52.clone.1, s32[]{:T(128)S(6)} %select_n.54, s32[]{:T(128)} %constant.52.clone.1) | dynamic-update-slice | bytes 131076 | tf_op jit(solution)/shard_map/dynamic_update_slice | solution.py:25
  218.1 42.0 %dynamic_update_slice.15 = bf16[2,2,4,128,64]{3,2,4,1,0:T(4,128)(2,1)S(1)} dynamic-update-slice(bf16[2,2,4,128,64]{3,2,4,1,0:T(4,128)(2,1)S(1)} %dynamic_update_slice.14, bf16[2,2,4,32,64]{3,2,4,1,0:T(4,128)(2,1)S(1)} %copy.76, s32[]{:T(128)} %constant.52.clone.1, s32[]{:T(128)} %constant.52.clone.1, s32[]{:T(128)} %constant.52.clone.1, s32[]{:T(128)S(6)} %select_n.56, s32[]{:T(128)} %constant.52.clone.1) | dynamic-update-slice | bytes 131076 | tf_op jit(solution)/shard_map/dynamic_update_slice | solution.py:20
  260.3 2.2 fusion.17
  262.7 4.2 %fusion.13 = f32[2,2,512,512]{3,2,1,0:T(8,128)S(1)} fusion(bf16[2,2,512,512]{3,2,1,0:T(8,128)(2,1)} %bitcast.76, f32[2,2,512,512]{3,2,1,0:T(8,128)} %mul.51, bf16[2,2,512,512]{3,2,1,0:T(8,128)(2,1)S(1)} %copy-done.2), kind=kOutput, calls=%fused_computation.36 | convolution fusion | flops 1076887552 | bytes 12582912 | tf_op jit(solution)/shard_map/vmap(vmap())/dot_general | solution.py:47
  272.0 3.9 %all-to-all-start.2 = ((bf16[4,2,256]{2,1,0:T(2,128)(2,1)}), bf16[4,2,256]{2,1,0:T(2,128)(2,1)S(1)}, u32[]{:S(2)}, u32[]{:S(2)}) async-start(bf16[4,2,256]{2,1,0:T(2,128)(2,1)} %reshape.135), calls=%async_computation.2 | async-start | bytes 8192 | tf_op jit(solution)/shard_map/all_to_all | solution.py:120
  275.8 7.2 %fusion.5 = f32[2,2,512,512]{3,2,1,0:T(8,128)} fusion(f32[2,2,512,512]{2,3,1,0:T(8,128)} %copy-done.1, f32[2,2,512]{2,1,0:T(2,128)S(1)} %get-tuple-element.20, pred[2,512]{1,0:T(4,128)(4,1)S(1)} %copy-done.7, f32[2,2,512,512]{3,2,1,0:T(8,128)} %mul.51, bf16[2,2,512,512]{3,2,1,0:T(8,128)(2,1)S(1)} %copy-done.2), kind=kOutput, calls=%fused_computation.13 | convolution fusion | flops 1080033280 | bytes 14689280 | tf_op jit(solution)/shard_map/vmap(vmap())/dot_general | solution.py:66
  284.0 5.1 %all-to-all-start = ((bf16[4,2,256]{2,1,0:T(2,128)(2,1)}), bf16[4,2,256]{2,1,0:T(2,128)(2,1)S(1)}, u32[]{:S(2)}, u32[]{:S(2)}) async-start(bf16[4,2,256]{2,1,0:T(2,128)(2,1)} %reshape.133), calls=%async_computation | async-start | bytes 8192 | tf_op jit(solution)/shard_map/all_to_all | solution.py:119
  289.0 3.0 add_convert_fusion
  292.0 3.0 copy.79
  295.0 5.1 %all-to-all-start.1 = ((bf16[1,2,2,4,128,512]{5,3,2,1,0,4:T(4,128)(2,1)}), bf16[1,2,2,4,128,512]{5,3,2,1,0,4:T(4,128)(2,1)S(1)}, u32[]{:S(2)}, u32[]{:S(2)}) async-start(bf16[1,2,2,4,128,512]{5,3,2,1,0,4:T(4,128)(2,1)} %copy.79), calls=%async_computation.1 | async-start | bytes 4194304 | tf_op jit(solution)/shard_map/all_to_all | solution.py:118
  301.4 3.1 copy.83
  305.7 40.6 %all-to-all-done.1 = bf16[1,2,2,4,128,512]{5,3,2,1,0,4:T(4,128)(2,1)S(1)} async-done(((bf16[1,2,2,4,128,512]{5,3,2,1,0,4:T(4,128)(2,1)}), bf16[1,2,2,4,128,512]{5,3,2,1,0,4:T(4,128)(2,1)S(1)}, u32[]{:S(2)}, u32[]{:S(2)}) %all-to-all-start.1) | async-done | bytes 2097184 | tf_op jit(solution)/shard_map/all_to_all | solution.py:118
  (74 shorter events, 28.9 us)
Async XLA Ops:
  7.2 253.1 %copy-start = (bf16[2,2,4,512]{3,2,1,0:T(4,128)(2,1)S(1)}, bf16[2,2,4,512]{3,2,1,0:T(4,128)(2,1)}, u32[]{:S(2)}) copy-start(bf16[2,2,4,512]{3,2,1,0:T(4,128)(2,1)} %param.14) | copy-start | bytes 49156
  7.2 18.8 %copy-start.2 = (bf16[2,2,512,512]{3,2,1,0:T(8,128)(2,1)S(1)}, bf16[2,2,512,512]{3,2,1,0:T(8,128)(2,1)}, u32[]{:S(2)}) copy-start(bf16[2,2,512,512]{3,2,1,0:T(8,128)(2,1)} %param.8) | copy-start | bytes 6291460
  7.2 253.1 %all-gather.2.cloned.1.call-start = ((), (), s32[]{:S(2)}) async-start(), calls=%async_computation.6 | async-start | bytes 2621440 | tf_op jit(solution)/shard_map/all_gather | solution.py:92
  10.6 11.9 %all-to-all-start.4 = ((bf16[2,2,128,4,4]{2,4,1,0,3:T(4,128)(2,1)}), bf16[2,2,128,4,4]{2,4,1,0,3:T(4,128)(2,1)S(1)}, u32[]{:S(2)}, u32[]{:S(2)}) async-start(bf16[2,2,128,4,4]{2,4,1,0,3:T(4,128)(2,1)} %copy.84), calls=%async_computation.4 | async-start | bytes 32768 | tf_op jit(solution)/shard_map/all_to_all | solution.py:103
  22.5 7.6 %copy-start.8 = (bf16[2,2,128,4,4]{2,4,1,0,3:T(4,128)(2,1)}, bf16[2,2,128,4,4]{2,4,1,0,3:T(4,128)(2,1)S(1)}, u32[]{:S(2)}) copy-start(bf16[2,2,128,4,4]{2,4,1,0,3:T(4,128)(2,1)S(1)} %all-to-all-done.4) | copy-start | bytes 49156
  22.5 19.8 %all-to-all-start.5 = ((bf16[2,2,128,4,64]{2,4,1,0,3:T(8,128)(2,1)}), bf16[2,2,128,4,64]{2,4,1,0,3:T(8,128)(2,1)S(1)}, u32[]{:S(2)}, u32[]{:S(2)}) async-start(bf16[2,2,128,4,64]{2,4,1,0,3:T(8,128)(2,1)} %copy.87), calls=%async_computation.5 | async-start | bytes 524288 | tf_op jit(solution)/shard_map/all_to_all | solution.py:104
  28.1 18.7 %copy-start.6 = (bf16[2,2,4,32,64]{4,3,2,1,0:T(8,128)(2,1)S(1)}, bf16[2,2,4,32,64]{4,3,2,1,0:T(8,128)(2,1)}, u32[]{:S(2)}) copy-start(bf16[2,2,4,32,64]{4,3,2,1,0:T(8,128)(2,1)} %param.13) | copy-start | bytes 196612
  28.1 22.6 %copy-start.12 = (s32[2]{0:T(128)S(1)}, s32[2]{0:T(128)}, u32[]{:S(2)}) copy-start(s32[2]{0:T(128)} %param.11) | copy-start | bytes 28
  42.3 70.6 %copy-start.4 = (bf16[2,2,128,4,64]{2,4,1,0,3:T(8,128)(2,1)}, bf16[2,2,128,4,64]{2,4,1,0,3:T(8,128)(2,1)S(1)}, u32[]{:S(2)}) copy-start(bf16[2,2,128,4,64]{2,4,1,0,3:T(8,128)(2,1)S(1)} %all-to-all-done.5) | copy-start | bytes 786436
  42.3 229.6 %all-to-all-start.3 = ((bf16[2,2,128,4,512]{4,2,1,0,3:T(8,128)(2,1)}), bf16[2,2,128,4,512]{4,2,1,0,3:T(8,128)(2,1)}, u32[]{:S(2)}, u32[]{:S(2)}) async-start(bf16[2,2,128,4,512]{4,2,1,0,3:T(8,128)(2,1)} %copy.82), calls=%async_computation.3 | async-start | bytes 4194304 | tf_op jit(solution)/shard_map/all_to_all | solution.py:102
  46.8 53.6 %collective-permute-start = (bf16[2,2,4,32,64]{4,3,2,1,0:T(8,128)(2,1)S(1)}, bf16[2,2,4,32,64]{4,3,2,1,0:T(8,128)(2,1)}, u32[]{:S(2)}, u32[]{:S(2)}) collective-permute-start(bf16[2,2,4,32,64]{4,3,2,1,0:T(8,128)(2,1)S(1)} %copy-done.6), channel_id=1, source_target_pairs={{0,4},{4,8},{8,12},{12,0},{1,5},{5,9},{9,13},{13,1},{2,6},{6,10},{... | collective-permute-start | bytes 196616 | tf_op jit(solution)/shard_map/ppermute | solution.py:19
  48.8 125.1 %collective-permute-start.1 = (bf16[2,2,4,32,64]{4,3,2,1,0:T(8,128)(2,1)S(1)}, bf16[2,2,4,32,64]{4,3,2,1,0:T(8,128)(2,1)}, u32[]{:S(2)}, u32[]{:S(2)}) collective-permute-start(bf16[2,2,4,32,64]{4,3,2,1,0:T(8,128)(2,1)S(1)} %copy-done.6), channel_id=1, source_target_pairs={{0,12},{4,0},{8,4},{12,8},{1,13},{5,1},{9,5},{13,9},{2,14},{6,2},{... | collective-permute-start | bytes 196616 | tf_op jit(solution)/shard_map/ppermute | solution.py:24
  100.4 116.6 %collective-permute-start.2 = (bf16[2,2,4,32,64]{4,3,2,1,0:T(8,128)(2,1)}, bf16[2,2,4,32,64]{4,3,2,1,0:T(8,128)(2,1)}, u32[]{:S(2)}, u32[]{:S(2)}) collective-permute-start(bf16[2,2,4,32,64]{4,3,2,1,0:T(8,128)(2,1)} %collective-permute-done), channel_id=1, source_target_pairs={{0,4},{4,8},{8,12},{12,0},{1,5},{5,9},{9,13},{13,1},{2,6},{6,10},{... | collective-permute-start | bytes 196616 | tf_op jit(solution)/shard_map/ppermute | solution.py:19
  123.2 139.3 %copy-start.10 = (pred[512,4]{0,1:T(4,128)(4,1)S(1)}, pred[512,4]{0,1:T(4,128)(4,1)}, u32[]{:S(2)}) copy-start(pred[512,4]{0,1:T(4,128)(4,1)} %fusion.8) | copy-start | bytes 6148
  123.2 139.3 %copy-start.11 = (bf16[2,2,4,64]{3,2,1,0:T(4,128)(2,1)S(1)}, bf16[2,2,4,64]{3,2,1,0:T(4,128)(2,1)}, u32[]{:S(2)}) copy-start(bf16[2,2,4,64]{3,2,1,0:T(4,128)(2,1)} %param.15) | copy-start | bytes 6148
  262.7 4.2 %copy-start.3 = (bf16[2,2,512,64]{2,3,1,0:T(8,128)(2,1)S(1)}, bf16[2,2,512,64]{2,3,1,0:T(8,128)(2,1)}, u32[]{:S(2)}) copy-start(bf16[2,2,512,64]{2,3,1,0:T(8,128)(2,1)} %param.10) | copy-start | bytes 786436
  262.7 4.2 %copy-start.7 = (pred[2,512]{1,0:T(4,128)(4,1)S(1)}, pred[2,512]{1,0:T(4,128)(4,1)}, u32[]{:S(2)}) copy-start(pred[2,512]{1,0:T(4,128)(4,1)} %broadcast_compare_fusion) | copy-start | bytes 3076
  268.2 2.0 copy-start.1
  272.0 12.0 %all-to-all-start.2 = ((bf16[4,2,256]{2,1,0:T(2,128)(2,1)}), bf16[4,2,256]{2,1,0:T(2,128)(2,1)S(1)}, u32[]{:S(2)}, u32[]{:S(2)}) async-start(bf16[4,2,256]{2,1,0:T(2,128)(2,1)} %reshape.135), calls=%async_computation.2 | async-start | bytes 8192 | tf_op jit(solution)/shard_map/all_to_all | solution.py:120
  284.0 11.0 %all-to-all-start = ((bf16[4,2,256]{2,1,0:T(2,128)(2,1)}), bf16[4,2,256]{2,1,0:T(2,128)(2,1)S(1)}, u32[]{:S(2)}, u32[]{:S(2)}) async-start(bf16[4,2,256]{2,1,0:T(2,128)(2,1)} %reshape.133), calls=%async_computation | async-start | bytes 8192 | tf_op jit(solution)/shard_map/all_to_all | solution.py:119
  292.0 8.1 %copy-start.9 = (bf16[2,2,128,4,4]{2,4,1,0,3:T(4,128)(2,1)S(1)}, bf16[2,2,128,4,4]{2,4,1,0,3:T(4,128)(2,1)}, u32[]{:S(2)}) copy-start(bf16[2,2,128,4,4]{2,4,1,0,3:T(4,128)(2,1)} %copy-done.8) | copy-start | bytes 49156
  292.0 8.7 %copy-start.5 = (bf16[2,2,128,4,64]{2,4,1,0,3:T(8,128)(2,1)S(1)}, bf16[2,2,128,4,64]{2,4,1,0,3:T(8,128)(2,1)}, u32[]{:S(2)}) copy-start(bf16[2,2,128,4,64]{2,4,1,0,3:T(8,128)(2,1)} %copy-done.4) | copy-start | bytes 786436
  295.0 51.3 %all-to-all-start.1 = ((bf16[1,2,2,4,128,512]{5,3,2,1,0,4:T(4,128)(2,1)}), bf16[1,2,2,4,128,512]{5,3,2,1,0,4:T(4,128)(2,1)S(1)}, u32[]{:S(2)}, u32[]{:S(2)}) async-start(bf16[1,2,2,4,128,512]{5,3,2,1,0,4:T(4,128)(2,1)} %copy.79), calls=%async_computation.1 | async-start | bytes 4194304 | tf_op jit(solution)/shard_map/all_to_all | solution.py:118
Sparse Core Ops, SparseCore 0:
  9.6 73.4 all-gather.1
